TPU v7x, 32 devices: a whole 2x2x4 slice. The times are simulated.
32 devices in a mesh: dom: 2 (over y), wide: 16 (over z, x, core).
Axes of the slice: x: 2, y: 2, z: 4, core: 2. Of those that a mesh axis runs over, the one named last changes fastest.
Arguments:
- embeddings: bfloat16 [16384, 768], P(('dom', 'wide')), parts along dimension 0, may hold values from -6 to 6
- cluster_id: int32 [16384, 1], P(('dom', 'wide')), parts along dimension 0, may hold values from 0 to 7; in each aligned block of 512 rows (0 to 511, 512 to 1023, ...) at most 160 rows name the same one
Outputs:
- max_similarity: float32 [16384], P(('dom', 'wide')), parts along dimension 0
There are 2 independent parts, one for each index of `dom`. A program takes and returns all parts, laid end to end along the dimension named above; each array names one. Nothing has to cross between parts.
Inputs may be any that keep to these rules, and one draw needn't show every extreme that they name: `cluster_id`: among the 512 rows of one device (aligned blocks of 512 rows), no cluster appears more than 160 times; every cluster has some row.
All inputs are finite; a program needn't handle non-finite values.
Results may differ from a plain program's by a relative error of at most 0.0014.
Values may be sent and summed in bfloat16 or wider, within the bound.
A program may use at most 64 MiB of HBM per device.

v0:
```python
import math

import jax
import jax.numpy as jnp
from jax import lax
from jax.sharding import PartitionSpec as P


def swapped(value, axis, bit):
    mask = 2**bit
    pairs = [(source, source ^ mask) for source in range(lax.axis_size(axis))]
    return lax.ppermute(value, axis, pairs)


def normalize(embedded):
    values = embedded.astype(jnp.float32)
    inverse = lax.rsqrt(jnp.mean(values * values, axis=1, keepdims=True) + 1e-06)
    return (values * inverse * (1.0 / math.sqrt(values.shape[1]))).astype(jnp.bfloat16)


def pair_scores(queries, key_rows):
    return jnp.einsum("qd,kd->qk", queries, key_rows, preferred_element_type=jnp.float32)


def masked_max(scores, allowed):
    return jnp.max(jnp.where(allowed, scores, -1.0), axis=1)


def per_device(embeddings, cluster_id):
    axis_size = lax.axis_size("wide")
    rows_dev = embeddings.shape[0]
    feature_dim = embeddings.shape[1]
    clusters = axis_size // 2
    capacity = (5 * rows_dev + 2 * axis_size - 1) // (2 * axis_size)
    buffer_rows = axis_size * capacity
    unit_rows = normalize(embeddings)
    labels = cluster_id[:, 0]
    my_index = lax.axis_index("wide")
    my_flip = my_index % 2
    position = lax.iota(jnp.int32, rows_dev)
    same_cluster = labels[:, None] == labels[None, :]
    earlier = position[None, :] < position[:, None]
    local_rank = jnp.sum((same_cluster & earlier).astype(jnp.int32), axis=1)
    target = 2 * labels + (local_rank + my_flip) % 2
    slot_index = target * capacity + local_rank // 2
    outgoing = jnp.zeros((buffer_rows, feature_dim), jnp.bfloat16).at[slot_index].set(unit_rows)
    cluster_count = jnp.sum(
        (labels[:, None] == lax.iota(jnp.int32, clusters)[None, :]).astype(jnp.int32), axis=0
    )
    parity = lax.iota(jnp.int32, axis_size) % 2
    send_count = (jnp.repeat(cluster_count, 2) + 1 - (parity + my_flip) % 2) // 2
    outgoing_blocks = outgoing.reshape(axis_size, capacity, feature_dim)
    count_blocks = send_count.reshape(axis_size, 1)
    received, counts = (
        lax.all_to_all(outgoing_blocks, "wide", split_axis=0, concat_axis=0, tiled=True),
        lax.all_to_all(count_blocks, "wide", split_axis=0, concat_axis=0, tiled=True),
    )
    own_rows = received.reshape(buffer_rows, feature_dim)
    partner, partner_counts = swapped((own_rows, counts), "wide", 0)
    side_bit = my_index % 2
    slot_pos = lax.iota(jnp.int32, capacity)
    sources = lax.iota(jnp.int32, axis_size)
    base_key = (sources[:, None] * (2 * capacity) + 2 * slot_pos[None, :]).reshape(-1)
    source_parity = jnp.repeat(sources % 2, capacity)
    own_key = base_key + (side_bit + source_parity) % 2
    partner_key = base_key + (1 - side_bit + source_parity) % 2
    own_live = (slot_pos[None, :] < counts).reshape(-1)
    partner_live = (slot_pos[None, :] < partner_counts).reshape(-1)
    blocks = 8
    query_rows = own_rows.reshape(blocks, -1, feature_dim)
    query_key = own_key.reshape(blocks, -1)

    def self_max(pieces):
        queries, keys_here = pieces
        return masked_max(
            pair_scores(queries, own_rows),
            own_live[None, :] & (own_key[None, :] < keys_here[:, None]),
        )

    self_best = lax.map(self_max, (query_rows, query_key)).reshape(-1)
    first = side_bit == 0
    left_rows = jnp.where(first, own_rows, partner)
    left_key = jnp.where(first, own_key, partner_key)
    left_live = jnp.where(first, own_live, partner_live)
    right_rows = jnp.where(first, partner, own_rows)
    right_key = jnp.where(first, partner_key, own_key)
    right_live = jnp.where(first, partner_live, own_live)
    half_rows = buffer_rows // 2
    start = side_bit * half_rows
    lower_rows = lax.dynamic_slice_in_dim(left_rows, start, half_rows, 0).reshape(
        blocks // 2, -1, feature_dim
    )
    lower_key = lax.dynamic_slice_in_dim(left_key, start, half_rows, 0).reshape(blocks // 2, -1)
    lower_live = lax.dynamic_slice_in_dim(left_live, start, half_rows, 0).reshape(blocks // 2, -1)

    def cross_max(pieces):
        queries, keys_here, live_here = pieces
        scores = pair_scores(queries, right_rows)
        row_best = masked_max(
            scores, right_live[None, :] & (right_key[None, :] < keys_here[:, None])
        )
        column_mask = live_here[:, None] & (keys_here[:, None] < right_key[None, :])
        column_best = jnp.max(jnp.where(column_mask, scores, -1.0), axis=0)
        return (row_best, column_best)

    row_best, column_best = lax.map(cross_max, (lower_rows, lower_key, lower_live))
    row_best = row_best.reshape(-1)
    column_best = jnp.max(column_best, axis=0)
    placed = lax.dynamic_update_slice_in_dim(
        jnp.full((buffer_rows,), -1.0, jnp.float32), row_best, start, 0
    )
    kept = jnp.where(first, placed, column_best)
    handed = jnp.where(first, column_best, placed)
    returned = swapped(handed, "wide", 0)
    best_all = jnp.maximum(self_best, jnp.maximum(kept, returned))
    back = lax.all_to_all(
        best_all.reshape(axis_size, capacity), "wide", split_axis=0, concat_axis=0, tiled=True
    )
    return back.reshape(-1)[slot_index]


def solution(mesh):
    placed = (P(("dom", "wide"), None), P(("dom", "wide"), None))
    return jax.shard_map(
        per_device, mesh=mesh, in_specs=placed, out_specs=P(("dom", "wide")), check_vma=False
    )
```

profile of v0, /device:TPU:0, one launch (start us, length us, event | category | flops | bytes accessed | tf_op | source)
XLA Modules:
  0.0 119.5 jit_solution(761466265437939160)
XLA Ops:
  0.0 1.0 convert_reduce_fusion
  1.0 1.4 %fusion.24 = f32[512]{0:T(512)S(1)} fusion(bf16[512,768]{1,0:T(8,128)(2,1)} %param.6), kind=kLoop, calls=%fused_computation.45 | loop fusion | flops 1179136 | bytes 788480 | tf_op jit(solution)/shard_map/reduce_sum | solution.py:17
  2.4 0.7 compare_select_fusion
  3.1 4.7 %scatter_custom_fusion = bf16[1280,768]{1,0:T(8,128)(2,1)} fusion(s32[512]{0:T(512)S(1)} %bitcast.57, bf16[]{:T(256)} %constant.137.clone.1, bf16[512,768]{1,0:T(8,128)(2,1)} %param.6, f32[]{:T(128)} %constant.146.clone.1, f32[512]{0:T(512)S(1)} %add_rsqrt_fusion), kind=kCustom, calls=%fused_computation.52 | custom fusion | flops 1572864 | bytes 2754566 | tf_op jit(solution)/shard_map/scatter | solution.py:46
  7.8 7.5 %all-to-all-start.1 = ((bf16[16,80,768]{2,1,0:T(8,128)(2,1)}), bf16[16,80,768]{2,1,0:T(8,128)(2,1)S(1)}, u32[]{:S(2)}, u32[]{:S(2)}) async-start(bf16[16,80,768]{2,1,0:T(8,128)(2,1)} %bitcast.46), calls=%async_computation.1 | async-start | bytes 3932160 | tf_op jit(solution)/shard_map/all_to_all | solution.py:55
  15.7 0.1 convert_reduce_fusion.1
  16.0 0.7 copy.5
  16.7 37.4 %all-to-all-done.1 = bf16[16,80,768]{2,1,0:T(8,128)(2,1)S(1)} async-done(((bf16[16,80,768]{2,1,0:T(8,128)(2,1)}), bf16[16,80,768]{2,1,0:T(8,128)(2,1)S(1)}, u32[]{:S(2)}, u32[]{:S(2)}) %all-to-all-start.1) | async-done | bytes 1966112 | tf_op jit(solution)/shard_map/all_to_all | solution.py:55
  54.0 10.7 %all-to-all-start = ((s32[16,1,1]{2,1,0:T(1,128)}), s32[16,1,1]{2,1,0:T(1,128)S(1)}, u32[]{:S(2)}, u32[]{:S(2)}) async-start(s32[16,1,1]{2,1,0:T(1,128)} %copy.5), calls=%async_computation | async-start | bytes 16384 | tf_op jit(solution)/shard_map/all_to_all | solution.py:56
  64.7 0.4 collective-permute-start.1
  65.9 5.3 %all-to-all-done = s32[16,1,1]{2,1,0:T(1,128)S(1)} async-done(((s32[16,1,1]{2,1,0:T(1,128)}), s32[16,1,1]{2,1,0:T(1,128)S(1)}, u32[]{:S(2)}, u32[]{:S(2)}) %all-to-all-start) | async-done | bytes 96 | tf_op jit(solution)/shard_map/all_to_all | solution.py:56
  71.2 0.4 reduce.1
  71.7 1.1 collective-permute-done
  72.8 0.1 select_n.191
  73.1 3.0 %broadcast_select_fusion = bf16[1280,768]{1,0:T(8,128)(2,1)} fusion(bf16[1280,768]{1,0:T(8,128)(2,1)} %collective-permute-done.1, pred[]{:T(512)} %eq.50, bf16[16,80,768]{2,1,0:T(8,128)(2,1)S(1)} %all-to-all-done.1), kind=kLoop, calls=%fused_computation.44 | loop fusion | flops 983040 | bytes 5898241 | tf_op jit(solution)/shard_map/jit(_where)/select_n | solution.py:85
  76.1 1.4 %dynamic-slice_select_fusion = bf16[640,768]{1,0:T(8,128)(2,1)S(1)} fusion(bf16[1280,768]{1,0:T(8,128)(2,1)} %collective-permute-done.1, s32[]{:T(128)S(6)} %select_n.186, bf16[1280,768]{1,0:T(8,128)(2,1)S(1)} %bitcast.41, pred[]{:T(512)} %eq.50), kind=kLoop, calls=%fused_computation.51 | loop fusion | flops 491520 | bytes 2949125 | tf_op jit(solution)/shard_map/jit(_where)/select_n | solution.py:82
  77.6 13.4 %while.26 = (s32[]{:T(128)}, f32[4,160]{1,0:T(4,128)S(1)}, f32[4,1280]{1,0:T(4,128)S(1)}, s32[4,160]{1,0:T(4,128)S(1)}, bf16[4,160,768]{2,1,0:T(8,128)(2,1)S(1)}...) while((s32[]{:T(128)}, f32[4,160]{1,0:T(4,128)S(1)}, ...), condition=%wide.region_10.11_spmd.clone.clone, body=%wide.region_7.10_spmd.clone.clone.sunk | while | flops 316246880 | bytes 2323947 | solution.py:106
  78.2 0.1 select_n.336
  78.3 2.5 %select_reduce_fusion.3 = (f32[1280]{0:T(1024)S(1)}, f32[160]{0:T(256)S(1)}) fusion(s32[1280]{0:T(1024)S(1)} %fusion.69, s32[160]{0:T(256)S(1)} %bitcast.54, pred[160]{0:T(512)(128)(4,1)S(1)} %dynamic-slice_reduce_fusion.2, pred[1280]{0:T(1024)(128)(4,1)S(1)} %select_n.336, bf16[1280,768]{1,0:T(8,128)(2,1)} %get-tuple-element.460, ...), kind=kOutput, calls=%fused_computation.19.clone.1 | convolution fusion | flops 316209760 | bytes 2229380 | tf_op jit(solution)/shard_map/while/body/eval_jaxpr/qd,kd->qk/dot_general | solution.py:22
  81.5 0.1 select_n.336
  81.6 2.5 %select_reduce_fusion.3 = (f32[1280]{0:T(1024)S(1)}, f32[160]{0:T(256)S(1)}) fusion(s32[1280]{0:T(1024)S(1)} %fusion.69, s32[160]{0:T(256)S(1)} %bitcast.54, pred[160]{0:T(512)(128)(4,1)S(1)} %dynamic-slice_reduce_fusion.2, pred[1280]{0:T(1024)(128)(4,1)S(1)} %select_n.336, bf16[1280,768]{1,0:T(8,128)(2,1)} %get-tuple-element.460, ...), kind=kOutput, calls=%fused_computation.19.clone.1 | convolution fusion | flops 316209760 | bytes 2229380 | tf_op jit(solution)/shard_map/while/body/eval_jaxpr/qd,kd->qk/dot_general | solution.py:22
  84.9 0.1 select_n.336
  85.0 2.5 %select_reduce_fusion.3 = (f32[1280]{0:T(1024)S(1)}, f32[160]{0:T(256)S(1)}) fusion(s32[1280]{0:T(1024)S(1)} %fusion.69, s32[160]{0:T(256)S(1)} %bitcast.54, pred[160]{0:T(512)(128)(4,1)S(1)} %dynamic-slice_reduce_fusion.2, pred[1280]{0:T(1024)(128)(4,1)S(1)} %select_n.336, bf16[1280,768]{1,0:T(8,128)(2,1)} %get-tuple-element.460, ...), kind=kOutput, calls=%fused_computation.19.clone.1 | convolution fusion | flops 316209760 | bytes 2229380 | tf_op jit(solution)/shard_map/while/body/eval_jaxpr/qd,kd->qk/dot_general | solution.py:22
  88.2 0.1 select_n.336
  88.3 2.5 %select_reduce_fusion.3 = (f32[1280]{0:T(1024)S(1)}, f32[160]{0:T(256)S(1)}) fusion(s32[1280]{0:T(1024)S(1)} %fusion.69, s32[160]{0:T(256)S(1)} %bitcast.54, pred[160]{0:T(512)(128)(4,1)S(1)} %dynamic-slice_reduce_fusion.2, pred[1280]{0:T(1024)(128)(4,1)S(1)} %select_n.336, bf16[1280,768]{1,0:T(8,128)(2,1)} %get-tuple-element.460, ...), kind=kOutput, calls=%fused_computation.19.clone.1 | convolution fusion | flops 316209760 | bytes 2229380 | tf_op jit(solution)/shard_map/while/body/eval_jaxpr/qd,kd->qk/dot_general | solution.py:22
  91.1 0.3 dynamic_update_slice.15
  91.4 11.8 %while.25 = (s32[]{:T(128)}, f32[8,160]{1,0:T(8,128)S(1)}, s32[8,160]{1,0:T(8,128)S(1)}, bf16[8,160,768]{2,1,0:T(8,128)(2,1)S(1)}, bf16[1280,768]{1,0:T(8,128)(2...) while((s32[]{:T(128)}, f32[8,160]{1,0:T(8,128)S(1)}, ...), condition=%wide.region_6.7_spmd.clone, body=%wide.region_4.6_spmd.clone.sunk | while | flops 315409760 | bytes 2276857 | solution.py:80
  91.8 0.1 and.250
  91.9 0.9 fusion.67
  93.3 0.1 and.250
  93.4 0.9 fusion.67
  94.8 0.1 and.250
  94.9 0.9 fusion.67
  96.3 0.1 and.250
  96.4 0.9 fusion.67
  97.8 0.1 and.250
  97.9 0.9 fusion.67
  99.2 0.1 and.250
  99.3 0.9 fusion.67
  100.8 0.9 fusion.67
  102.2 0.1 and.250
  102.3 0.9 fusion.67
  103.4 0.7 all_to_all.18
  104.1 3.5 %all-to-all-start.2 = ((f32[16,1,80]{2,1,0:T(1,128)}), f32[16,1,80]{2,1,0:T(1,128)S(1)}, u32[]{:S(2)}, u32[]{:S(2)}) async-start(f32[16,1,80]{2,1,0:T(1,128)} %all_to_all.18), calls=%async_computation.2 | async-start | bytes 16384 | tf_op jit(solution)/shard_map/all_to_all | solution.py:116
  107.6 6.4 %all-to-all-done.2 = f32[16,1,80]{2,1,0:T(1,128)S(1)} async-done(((f32[16,1,80]{2,1,0:T(1,128)}), f32[16,1,80]{2,1,0:T(1,128)S(1)}, u32[]{:S(2)}, u32[]{:S(2)}) %all-to-all-start.2) | async-done | bytes 5152 | tf_op jit(solution)/shard_map/all_to_all | solution.py:116
  114.0 0.5 broadcast.407
  114.5 0.7 reduce.7
  115.2 4.3 %gather_fusion = f32[512]{0:T(512)} fusion(f32[1280]{0:T(1024)S(1)} %reshape.313, s32[1024]{0:T(1024)S(1)} %pad_clamp_fusion), kind=kCustom, calls=%fused_computation | custom fusion | bytes 6144 | tf_op jit(solution)/shard_map/gather | solution.py:119
  (166 shorter events, 8.3 us)
Async XLA Ops:
  7.8 7.9 %copy-start = (s32[512,1]{0,1:T(1,128)S(1)}, s32[512,1]{0,1:T(1,128)}, u32[]{:S(2)}) copy-start(s32[512,1]{0,1:T(1,128)} %param.7) | copy-start | bytes 6148
  7.8 46.2 %all-to-all-start.1 = ((bf16[16,80,768]{2,1,0:T(8,128)(2,1)}), bf16[16,80,768]{2,1,0:T(8,128)(2,1)S(1)}, u32[]{:S(2)}, u32[]{:S(2)}) async-start(bf16[16,80,768]{2,1,0:T(8,128)(2,1)} %bitcast.46), calls=%async_computation.1 | async-start | bytes 3932160 | tf_op jit(solution)/shard_map/all_to_all | solution.py:55
  54.0 17.1 %all-to-all-start = ((s32[16,1,1]{2,1,0:T(1,128)}), s32[16,1,1]{2,1,0:T(1,128)S(1)}, u32[]{:S(2)}, u32[]{:S(2)}) async-start(s32[16,1,1]{2,1,0:T(1,128)} %copy.5), calls=%async_computation | async-start | bytes 16384 | tf_op jit(solution)/shard_map/all_to_all | solution.py:56
  64.7 8.4 %collective-permute-start.1 = (bf16[1280,768]{1,0:T(8,128)(2,1)S(1)}, bf16[1280,768]{1,0:T(8,128)(2,1)}, u32[]{:S(2)}, u32[]{:S(2)}) collective-permute-start(bf16[1280,768]{1,0:T(8,128)(2,1)S(1)} %bitcast.40), channel_id=1, source_target_pairs={{0,1},{1,0},{2,3},{3,2},{4,5},{5,4},{6,7},{7,6},{8,9},{9,8},{10,11... | collective-permute-start | bytes 5898248 | tf_op jit(solution)/shard_map/ppermute | solution.py:12
  71.5 1.2 %collective-permute-start = (s32[16,1]{0,1:T(1,128)S(1)}, s32[16,1]{0,1:T(1,128)S(1)}, u32[]{:S(2)}, u32[]{:S(2)}) collective-permute-start(s32[16,1]{0,1:T(1,128)S(1)} %bitcast.48), channel_id=1, source_target_pairs={{0,1},{1,0},{2,3},{3,2},{4,5},{5,4},{6,7},{7,6},{8,9},{9,8},{10,11... | collective-permute-start | bytes 200 | tf_op jit(solution)/shard_map/ppermute | solution.py:12
  91.3 12.0 %collective-permute-start.2 = (f32[1280]{0:T(1024)S(1)}, f32[1280]{0:T(1024)S(1)}, u32[]{:S(2)}, u32[]{:S(2)}) collective-permute-start(f32[1280]{0:T(1024)S(1)} %broadcast_select_fusion.1), channel_id=1, source_target_pairs={{0,1},{1,0},{2,3},{3,2},{4,5},{5,4},{6,7},{7,6},{8,9},{9,8},{10,11... | collective-permute-start | bytes 15368 | tf_op jit(solution)/shard_map/ppermute | solution.py:12
  104.1 9.9 %all-to-all-start.2 = ((f32[16,1,80]{2,1,0:T(1,128)}), f32[16,1,80]{2,1,0:T(1,128)S(1)}, u32[]{:S(2)}, u32[]{:S(2)}) async-start(f32[16,1,80]{2,1,0:T(1,128)} %all_to_all.18), calls=%async_computation.2 | async-start | bytes 16384 | tf_op jit(solution)/shard_map/all_to_all | solution.py:116
where the time goes:
time: 120 us; the launch traced here: 119 us
  waiting for transfers between devices  50.1 us (42%)
  starting transfers between devices  22.2 us (18%)
  matrix products  17.4 us (14%)
  other arithmetic  15.8 us (13%)
  local copies, waits for them, and re-layouts  13.3 us (11%)
    all_to_all x1, waiting for transfers between devices, per_device(): lax.all_to_all(outgoing_blocks, 'wide', split_axis=0, concat_axis=0, tile...  37.4 us
    dot_general x12, matrix products, pair_scores(): jnp.einsum('qd,kd->qk', queries, key_rows, preferred_element_type=jnp.flo...  17.4 us
    all_to_all x1, starting transfers between devices, per_device(): lax.all_to_all(count_blocks, 'wide', split_axis=0, concat_axis=0, tiled=T...  10.7 us
    all_to_all x1, starting transfers between devices, per_device(): lax.all_to_all(outgoing_blocks, 'wide', split_axis=0, concat_axis=0, tile...  7.52 us
    all_to_all x1, waiting for transfers between devices, per_device(): lax.all_to_all(best_all.reshape(axis_size, capacity), 'wide', split_axis=...  6.38 us
    all_to_all x1, waiting for transfers between devices, per_device(): lax.all_to_all(count_blocks, 'wide', split_axis=0, concat_axis=0, tiled=T...  5.28 us
    scatter x1, other arithmetic, per_device(): jnp.zeros((buffer_rows, feature_dim), jnp.bfloat16).at[slot_index]  4.71 us
    gather x1, local copies, waits for them, and re-layouts, per_device(): return back.reshape(-1)[slot_index]  4.27 us
  transfers between devices with their start and end apart: 6, of which 4 were waited for; matrix products, arithmetic and copies ran while one was open for 12% of the time, Pallas kernels for 0%

commit v1 on v0

--- a/solution.py
+++ b/solution.py
@@ -1,8 +1,11 @@
+import functools
 import math
 
 import jax
 import jax.numpy as jnp
 from jax import lax
+from jax.experimental import pallas as pl
+from jax.experimental.pallas import tpu as pltpu
 from jax.sharding import PartitionSpec as P
 
 
@@ -119,8 +122,304 @@
     return back.reshape(-1)[slot_index]
 
 
+LANES = 4
+CHUNK = 128
+MESH = pl.DeviceIdType.MESH
+
+
+def grid_kernel(levels, x_ref, id_ref, out_ref, lev, lev_id, unit, left, left_id, right, right_id,
+                acc, part, res, back, back_in, lev_send, lev_recv, left_send, left_recv,
+                right_send, right_recv, res_send, res_recv, back_send, back_recv):
+    me = lax.axis_index("wide")
+    lane = lax.rem(me, LANES)
+    level = me // LANES
+    base = level * LANES
+    half = levels // 2
+    rows, width = x_ref.shape
+    chunks = rows // CHUNK
+
+    def peer(slot):
+        low = lax.rem(lane, 2)
+        high = lane // 2
+        low = 1 - low if slot % 2 else low
+        high = 1 - high if slot // 2 else high
+        return base + 2 * high + low
+
+    right_dev = me + LANES
+    left_dev = me - LANES
+    has_right = level < levels - 1
+    sends_own = level < half
+    takes_back = level == half
+    gives_back = level == half + 1
+
+    barrier = pltpu.get_barrier_semaphore()
+    for slot in range(1, LANES):
+        pl.semaphore_signal(barrier, inc=1, device_id={"wide": peer(slot)}, device_id_type=MESH)
+
+    @pl.when(has_right)
+    def _():
+        pl.semaphore_signal(barrier, inc=1, device_id={"wide": right_dev}, device_id_type=MESH)
+
+    @pl.when(level > 0)
+    def _():
+        pl.semaphore_signal(barrier, inc=1, device_id={"wide": left_dev}, device_id_type=MESH)
+
+    peers = LANES - 1 + has_right.astype(jnp.int32) + (level > 0).astype(jnp.int32)
+    pl.semaphore_wait(barrier, peers)
+
+    def piece(block, ids, k):
+        return ids if k == chunks else block.at[pl.ds(k * CHUNK, CHUNK)]
+
+    order = [chunks] + list(range(chunks))
+
+    def send(src, src_id, dst, dst_id, k, ssem, rsem, dev):
+        return pltpu.make_async_remote_copy(
+            src_ref=piece(src, src_id, k), dst_ref=piece(dst, dst_id, k),
+            send_sem=ssem.at[k], recv_sem=rsem.at[k],
+            device_id={"wide": dev}, device_id_type=MESH)
+
+    def level_own(slot, k):
+        return send(x_ref, id_ref, lev.at[slot - 1], lev_id.at[slot - 1], k,
+                    lev_send.at[slot - 1], lev_recv.at[slot - 1], peer(slot))
+
+    def level_pass(k):
+        return send(lev.at[1], lev_id.at[1], lev.at[2], lev_id.at[2], k,
+                    lev_send.at[2], lev_recv.at[2], peer(1))
+
+    def right_own(k):
+        return send(x_ref, id_ref, left.at[0], left_id.at[0], k,
+                    left_send.at[0], left_recv.at[0], right_dev)
+
+    def right_pass(j, to, k):
+        return send(left.at[j], left_id.at[j], left.at[to], left_id.at[to], k,
+                    left_send.at[to], left_recv.at[to], right_dev)
+
+    def left_own(k):
+        return send(x_ref, id_ref, right, right_id, k, right_send, right_recv, left_dev)
+
+    for k in order:
+        @pl.when(sends_own & has_right)
+        def _(k=k):
+            right_own(k).start()
+
+        level_own(2, k).start()
+        level_own(1, k).start()
+
+        @pl.when(gives_back)
+        def _(k=k):
+            left_own(k).start()
+
+    def normal(block):
+        values = block.astype(jnp.float32)
+        inverse = lax.rsqrt(jnp.mean(values * values, axis=1, keepdims=True) + 1e-06)
+        return (values * inverse * (1.0 / math.sqrt(width))).astype(jnp.bfloat16)
+
+    def column(ids, k):
+        row = ids[:, k * CHUNK:(k + 1) * CHUNK]
+        return jnp.transpose(jnp.broadcast_to(row, (CHUNK, CHUNK)))[:, :1]
+
+    def scores(keys, queries):
+        return lax.dot_general(keys, queries, (((1,), (1,)), ((), ())),
+                               preferred_element_type=jnp.float32)
+
+    def fold(values):
+        count, wide_by = values.shape
+        return jnp.max(values.reshape(count // 8, 8, wide_by), axis=0)
+
+    def forward(j, k):
+        if j + 1 < left.shape[0]:
+            @pl.when(has_right & sends_own)
+            def _():
+                right_pass(j, j + 1, k).start()
+
+        @pl.when(has_right & jnp.logical_not(sends_own))
+        def _():
+            right_pass(j, j, k).start()
+
+    def ids_of(slot):
+        return id_ref if slot == 0 else lev_id.at[slot - 1]
+
+    def unit_chunk(slot, k):
+        at = pl.ds(k * CHUNK, CHUNK)
+        unit[slot, at, :] = normal(x_ref[at, :] if slot == 0 else lev[slot - 1, at, :])
+
+    acc[...] = jnp.full_like(acc, -1.0)
+    for k in range(chunks):
+        unit_chunk(0, k)
+
+    def own_level(slot):
+        ids = ids_of(slot)
+        best = acc[0]
+        for k in range(chunks):
+            value = scores(unit[slot, pl.ds(k * CHUNK, CHUNK), :], unit[0])
+            keep = column(ids[...], k) == id_ref[...]
+            if slot == 0:
+                key_at = lax.broadcasted_iota(jnp.int32, value.shape, 0) + k * CHUNK
+                keep = keep & (key_at < lax.broadcasted_iota(jnp.int32, value.shape, 1))
+            best = jnp.maximum(best, fold(jnp.where(keep, value, -1.0)))
+        acc[0] = best
+
+    own_level(0)
+    for k in order:
+        @pl.when(level > 0)
+        def _(k=k):
+            right_own(k).wait_recv()
+            forward(0, k)
+
+        level_own(2, k).wait_recv()
+        level_pass(k).start()
+        level_own(1, k).wait_recv()
+        if k < chunks:
+            unit_chunk(1, k)
+            unit_chunk(2, k)
+    for k in order:
+        level_pass(k).wait_recv()
+        if k < chunks:
+            unit_chunk(3, k)
+
+    for slot in range(1, LANES):
+        @pl.when(peer(slot) < me)
+        def _(slot=slot):
+            own_level(slot)
+
+    def from_left(j, k):
+        keys = normal(left[j, pl.ds(k * CHUNK, CHUNK), :])
+        ids = column(left_id[j], k)
+        for slot in range(LANES):
+            value = scores(keys, unit[slot])
+            value = jnp.where(ids == ids_of(slot)[...], value, -1.0)
+            acc[slot] = jnp.maximum(acc[slot], fold(value))
+
+    def from_right(k):
+        at = pl.ds(k * CHUNK, CHUNK)
+        queries = normal(right[at, :])
+        ids = right_id[:, k * CHUNK:(k + 1) * CHUNK]
+        best = jnp.full((8, CHUNK), -1.0, jnp.float32)
+        for slot in range(LANES):
+            for i in range(chunks):
+                value = scores(unit[slot, pl.ds(i * CHUNK, CHUNK), :], queries)
+                keep = column(ids_of(slot)[...], i) == ids
+                best = jnp.maximum(best, fold(jnp.where(keep, value, -1.0)))
+        back[:, k * CHUNK:(k + 1) * CHUNK] = jnp.max(best, axis=0, keepdims=True)
+
+    def back_copy():
+        return pltpu.make_async_remote_copy(
+            src_ref=back, dst_ref=back_in, send_sem=back_send, recv_sem=back_recv,
+            device_id={"wide": right_dev}, device_id_type=MESH)
+
+    for j in range(1, half):
+        for k in order:
+            @pl.when(level > j)
+            def _(j=j, k=k):
+                right_pass(j - 1, j, k).wait_recv()
+                forward(j, k)
+
+            if k < chunks:
+                @pl.when(level >= j)
+                def _(j=j, k=k):
+                    from_left(j - 1, k)
+
+            if j == half - 1:
+                @pl.when(takes_back & has_right)
+                def _(k=k):
+                    left_own(k).wait_recv()
+                    if k < chunks:
+                        from_right(k)
+
+                if k == chunks - 1:
+                    @pl.when(takes_back & has_right)
+                    def _():
+                        back_copy().start()
+
+                if k < chunks:
+                    @pl.when(level > j)
+                    def _(j=j, k=k):
+                        from_left(j, k)
+
+    def res_copy(slot):
+        return pltpu.make_async_remote_copy(
+            src_ref=part.at[slot - 1], dst_ref=res.at[slot - 1], send_sem=res_send.at[slot - 1],
+            recv_sem=res_recv.at[slot - 1], device_id={"wide": peer(slot)}, device_id_type=MESH)
+
+    for slot in (3, 2, 1):
+        part[slot - 1] = jnp.max(acc[slot], axis=0, keepdims=True)
+        res_copy(slot).start()
+    out_ref[...] = jnp.max(acc[0], axis=0, keepdims=True)
+
+    @pl.when(gives_back)
+    def _():
+        back_copy().wait_recv()
+        out_ref[...] = jnp.maximum(out_ref[...], back_in[...])
+
+    for slot in range(1, LANES):
+        res_copy(slot).wait_recv()
+        out_ref[...] = jnp.maximum(out_ref[...], res[slot - 1])
+
+    for slot in range(1, LANES):
+        res_copy(slot).wait_send()
+    for k in order:
+        level_own(2, k).wait_send()
+        level_own(1, k).wait_send()
+        level_pass(k).wait_send()
+
+        @pl.when(sends_own & has_right)
+        def _(k=k):
+            right_own(k).wait_send()
+
+        @pl.when(gives_back)
+        def _(k=k):
+            left_own(k).wait_send()
+
+        for j in range(half):
+            if j + 1 < half:
+                @pl.when(has_right & sends_own & (level > j))
+                def _(j=j, k=k):
+                    right_pass(j, j + 1, k).wait_send()
+
+            @pl.when(has_right & jnp.logical_not(sends_own))
+            def _(j=j, k=k):
+                right_pass(j, j, k).wait_send()
+
+    @pl.when(takes_back & has_right)
+    def _():
+        back_copy().wait_send()
+
+
+def grid_plan(levels, embeddings, cluster_id):
+    rows, width = embeddings.shape
+    half = levels // 2
+    pieces = rows // CHUNK + 1
+    bf16, i32, f32 = jnp.bfloat16, jnp.int32, jnp.float32
+    dma = pltpu.SemaphoreType.DMA
+    best = pl.pallas_call(
+        functools.partial(grid_kernel, levels),
+        out_shape=jax.ShapeDtypeStruct((1, rows), f32),
+        in_specs=[pl.BlockSpec(memory_space=pltpu.VMEM)] * 2,
+        out_specs=pl.BlockSpec(memory_space=pltpu.VMEM),
+        scratch_shapes=[
+            pltpu.VMEM((LANES - 1, rows, width), bf16), pltpu.VMEM((LANES - 1, 1, rows), i32),
+            pltpu.VMEM((LANES, rows, width), bf16),
+            pltpu.VMEM((half, rows, width), bf16), pltpu.VMEM((half, 1, rows), i32),
+            pltpu.VMEM((rows, width), bf16), pltpu.VMEM((1, rows), i32),
+            pltpu.VMEM((LANES, 8, rows), f32),
+            pltpu.VMEM((LANES - 1, 1, rows), f32), pltpu.VMEM((LANES - 1, 1, rows), f32),
+            pltpu.VMEM((1, rows), f32), pltpu.VMEM((1, rows), f32),
+            dma((LANES - 1, pieces)), dma((LANES - 1, pieces)),
+            dma((half, pieces)), dma((half, pieces)),
+            dma((pieces,)), dma((pieces,)),
+            dma((LANES - 1,)), dma((LANES - 1,)), dma, dma,
+        ],
+        compiler_params=pltpu.CompilerParams(
+            collective_id=0, has_side_effects=True, vmem_limit_bytes=40 * 2**20),
+    )(embeddings, cluster_id.reshape(1, rows))
+    return best.reshape(-1)
+
+
 def solution(mesh):
     placed = (P(("dom", "wide"), None), P(("dom", "wide"), None))
+    levels = mesh.shape["wide"] // LANES
+    fits = levels == 4 and mesh.shape["wide"] % LANES == 0
+    plan = functools.partial(grid_plan, levels) if fits else per_device
     return jax.shard_map(
-        per_device, mesh=mesh, in_specs=placed, out_specs=P(("dom", "wide")), check_vma=False
-    )
+        plan, mesh=mesh, in_specs=placed, out_specs=P(("dom", "wide")), check_vma=False
+    )

time: 120 us -> 52.2 us (0.43)
  the two profiles are of different devices: /device:TPU:0 before, /device:TPU:24 now
where the time goes in v1:
time: 52.2 us; the launch traced here: 52.1 us
  Pallas kernels  49.7 us (95%)
  local copies, waits for them, and re-layouts  2.39 us (5%)
    pallas_call x1, Pallas kernels, grid_plan(): pl.pallas_call(functools.partial(grid_kernel, levels), out_shape=jax.Shap...  49.7 us
    unnamed x5, local copies, waits for them, and re-layouts  2.39 us

profile of v1, /device:TPU:24, one launch (start us, length us, event | category | flops | bytes accessed | tf_op | source)
XLA Modules:
  0.0 52.1 jit_solution(9284258853321154694)
XLA Ops:
  0.0 0.0 copy-start
  0.0 1.1 %copy-done = bf16[512,768]{1,0:T(8,128)(2,1)S(1)} copy-done((bf16[512,768]{1,0:T(8,128)(2,1)S(1)}, bf16[512,768]{1,0:T(8,128)(2,1)}, u32[]{:S(2)}) %copy-start) | copy-done | bytes 786456
  1.1 0.0 copy-start.1
  1.1 0.7 %copy-done.1 = s32[512,1]{0,1:T(1,128)S(1)} copy-done((s32[512,1]{0,1:T(1,128)S(1)}, s32[512,1]{0,1:T(1,128)}, u32[]{:S(2)}) %copy-start.1) | copy-done | bytes 2072
  1.8 49.7 %shard_map.28 = f32[1,512]{1,0:T(1,128)S(1)} custom-call(bf16[512,768]{1,0:T(8,128)(2,1)S(1)} %copy-done, s32[1,512]{1,0:T(1,128)S(1)} %bitcast.3), custom_call_target="tpu_custom_call" | custom-call | tf_op jit(solution)/shard_map/pallas_call | solution.py:394
  51.5 0.6 %copy.4 = f32[512]{0:T(512)} copy(f32[512]{0:T(512)S(1)} %bitcast.2) | data formatting | bytes 4096
Async XLA Ops:
  0.0 1.1 %copy-start = (bf16[512,768]{1,0:T(8,128)(2,1)S(1)}, bf16[512,768]{1,0:T(8,128)(2,1)}, u32[]{:S(2)}) copy-start(bf16[512,768]{1,0:T(8,128)(2,1)} %x_ref.1) | copy-start | bytes 2359300
  1.1 0.7 %copy-start.1 = (s32[512,1]{0,1:T(1,128)S(1)}, s32[512,1]{0,1:T(1,128)}, u32[]{:S(2)}) copy-start(s32[512,1]{0,1:T(1,128)} %param.3) | copy-start | bytes 6148

commit v2 on v0

--- a/solution.py
+++ b/solution.py
@@ -1,8 +1,11 @@
+import functools
 import math
 
 import jax
 import jax.numpy as jnp
 from jax import lax
+from jax.experimental import pallas as pl
+from jax.experimental.pallas import tpu as pltpu
 from jax.sharding import PartitionSpec as P
 
 
@@ -119,8 +122,460 @@
     return back.reshape(-1)[slot_index]
 
 
+LANES = 4
+PIECE = 64
+CHUNK = 128
+MESH = pl.DeviceIdType.MESH
+
+
+def grid_kernel(levels, x_ref, id_ref, out_ref, lev, lev_id, unit, id_col, left, left_id, right,
+                right_id, ferry, relay, acc, query_best, part, res, back, back_in,
+                lev_send, lev_recv, left_send, left_recv, right_send, right_recv,
+                ferry_send, ferry_recv, relay_send, relay_recv, hand_send,
+                res_send, res_recv, back_send, back_recv):
+    plane = lax.axis_index("dom")
+    other = 1 - plane
+    me = lax.axis_index("wide")
+    lane = lax.rem(me, LANES)
+    place = me // LANES
+    base = place * LANES
+    half = levels // 2
+    rows, width = x_ref.shape
+    count = rows // PIECE
+    chunks = rows // CHUNK
+    up = plane == 0
+    level = jnp.where(up, place, levels - 1 - place)
+    step = jnp.where(up, LANES, -LANES)
+    relay_level = levels - 1 - level
+    detour = [p for p in range(count) if p % 2 and p > 1]
+    direct = [p for p in range(count) if p not in detour]
+
+    def at_level(wanted):
+        return me + (wanted - level) * step
+
+    def peer(slot):
+        low = lax.rem(lane, 2)
+        high = lane // 2
+        low = 1 - low if slot % 2 else low
+        high = 1 - high if slot // 2 else high
+        return base + 2 * high + low
+
+    has_next = level < levels - 1
+    sends_own = level < half
+    takes_back = level == half
+    gives_back = level == half + 1
+
+    barrier = pltpu.get_barrier_semaphore()
+    for slot in range(1, LANES):
+        pl.semaphore_signal(barrier, inc=1, device_id={"dom": plane, "wide": peer(slot)},
+                            device_id_type=MESH)
+    for far in range(1, levels):
+        there = lax.rem(place + far, levels) * LANES + lane
+        pl.semaphore_signal(barrier, inc=1, device_id={"dom": plane, "wide": there},
+                            device_id_type=MESH)
+    pl.semaphore_signal(barrier, inc=1, device_id={"dom": other, "wide": me}, device_id_type=MESH)
+    pl.semaphore_wait(barrier, LANES + levels - 1)
+
+    def piece(block, ids, p):
+        return ids if p == count else block.at[pl.ds(p * PIECE, PIECE)]
+
+    order = [count] + list(range(count))
+
+    def send(src, src_id, dst, dst_id, p, ssem, rsem, dev, row=None):
+        return pltpu.make_async_remote_copy(
+            src_ref=piece(src, src_id, p), dst_ref=piece(dst, dst_id, p),
+            send_sem=ssem.at[p], recv_sem=rsem.at[p],
+            device_id={"dom": plane if row is None else row, "wide": dev}, device_id_type=MESH)
+
+    def level_own(slot, p):
+        return send(x_ref, id_ref, lev.at[slot - 1], lev_id.at[slot - 1], p,
+                    lev_send.at[slot - 1], lev_recv.at[slot - 1], peer(slot))
+
+    def level_pass(p):
+        return send(lev.at[1], lev_id.at[1], lev.at[2], lev_id.at[2], p,
+                    lev_send.at[2], lev_recv.at[2], peer(1))
+
+    def next_own(p):
+        return send(x_ref, id_ref, left.at[0], left_id.at[0], p,
+                    left_send.at[0], left_recv.at[0], me + step)
+
+    def next_pass(j, to, p):
+        return send(left.at[j], left_id.at[j], left.at[to], left_id.at[to], p,
+                    left_send.at[to], left_recv.at[to], me + step)
+
+    def back_own(p):
+        return send(x_ref, id_ref, right, right_id, p, right_send, right_recv, me - step)
+
+    def ferry_out(p):
+        return send(x_ref, None, ferry, None, p, ferry_send, ferry_recv, me, other)
+
+    def relay_own(p):
+        return send(ferry, None, relay.at[0], None, p, relay_send.at[0], relay_recv.at[0],
+                    me - step)
+
+    def relay_pass(j, to, p):
+        return send(relay.at[j], None, relay.at[to], None, p, relay_send.at[to],
+                    relay_recv.at[to], me - step)
+
+    def hand(j, p):
+        return send(relay.at[j], None, left.at[j], None, p, hand_send.at[j], left_recv.at[j],
+                    me, other)
+
+    for p in order:
+        @pl.when(sends_own)
+        def _(p=p):
+            (ferry_out if p in detour else next_own)(p).start()
+
+        level_own(2, p).start()
+        level_own(1, p).start()
+
+        @pl.when(gives_back)
+        def _(p=p):
+            back_own(p).start()
+
+    def normal(block):
+        values = block.astype(jnp.float32)
+        inverse = lax.rsqrt(jnp.mean(values * values, axis=1, keepdims=True) + 1e-06)
+        return (values * inverse * (1.0 / math.sqrt(width))).astype(jnp.bfloat16)
+
+    def column(ids, k):
+        row = ids[:, k * CHUNK:(k + 1) * CHUNK]
+        return jnp.transpose(jnp.broadcast_to(row, (CHUNK, CHUNK)))
+
+    def scores(keys, queries):
+        return lax.dot_general(keys, queries, (((1,), (1,)), ((), ())),
+                               preferred_element_type=jnp.float32)
+
+    def fold(values):
+        tall, wide_by = values.shape
+        return jnp.max(values.reshape(tall // 8, 8, wide_by), axis=0)
+
+    def ids_of(slot):
+        return id_ref if slot == 0 else lev_id.at[slot - 1]
+
+    def unit_chunk(slot, k):
+        at = pl.ds(k * CHUNK, CHUNK)
+        unit[slot, at, :] = normal(x_ref[at, :] if slot == 0 else lev[slot - 1, at, :])
+        id_col[slot, at, :] = column(ids_of(slot), k)
+
+    def own_level(slot):
+        best = acc[0]
+        for k in range(chunks):
+            at = pl.ds(k * CHUNK, CHUNK)
+            value = scores(unit[slot, at, :], unit[0])
+            keep = id_col[slot, at, :][:, :1] == id_ref[...]
+            if slot == 0:
+                key_at = lax.broadcasted_iota(jnp.int32, value.shape, 0) + k * CHUNK
+                keep = keep & (key_at < lax.broadcasted_iota(jnp.int32, value.shape, 1))
+            best = jnp.maximum(best, fold(jnp.where(keep, value, -1.0)))
+        acc[0] = best
+
+    def earlier_level(slot):
+        @pl.when(peer(slot) < me)
+        def _():
+            own_level(slot)
+
+    def as_keys(block, ids, k, slots):
+        keys = normal(block[pl.ds(k * CHUNK, CHUNK), :])
+        key_ids = column(ids, k)[:, :1]
+        for slot in slots:
+            value = scores(keys, unit[slot])
+            value = jnp.where(key_ids == ids_of(slot)[...], value, -1.0)
+            acc[slot] = jnp.maximum(acc[slot], fold(value))
+
+    def as_queries(block, ids, best_at, k, slots):
+        queries = normal(block[pl.ds(k * CHUNK, CHUNK), :])
+        query_ids = ids[:, k * CHUNK:(k + 1) * CHUNK]
+        best = query_best[best_at, :, k * CHUNK:(k + 1) * CHUNK]
+        for slot in slots:
+            value = scores(unit[slot], queries)
+            value = jnp.where(id_col[slot] == query_ids, value, -1.0)
+            best = jnp.maximum(best, fold(value))
+        query_best[best_at, :, k * CHUNK:(k + 1) * CHUNK] = best
+
+    def from_left(j, k, slots):
+        @pl.when((level > j) & up)
+        def _():
+            as_keys(left.at[j], left_id.at[j], k, slots)
+
+        @pl.when((level > j) & jnp.logical_not(up))
+        def _():
+            as_queries(left.at[j], left_id.at[j], j, k, slots)
+
+    def from_right(k, slots):
+        @pl.when(takes_back & up)
+        def _():
+            as_queries(right, right_id, half, k, slots)
+
+        @pl.when(takes_back & jnp.logical_not(up))
+        def _():
+            as_keys(right, right_id, k, slots)
+
+    def left_wait(j, p):
+        (next_own(p) if j == 0 else next_pass(j - 1, j, p)).wait_recv()
+
+    def left_step(j, p):
+        @pl.when(level > j)
+        def _():
+            left_wait(j, p)
+            if j + 1 < half:
+                @pl.when(sends_own)
+                def _():
+                    next_pass(j, j + 1, p).start()
+
+            @pl.when(has_next & jnp.logical_not(sends_own))
+            def _():
+                next_pass(j, j, p).start()
+
+    def left_rest(j, k):
+        for p in detour:
+            if p * PIECE // CHUNK == k:
+                @pl.when(level > j)
+                def _(p=p):
+                    left_wait(j, p)
+
+    def ferry_step(p):
+        @pl.when(relay_level < half)
+        def _():
+            ferry_out(p).wait_recv()
+            relay_own(p).start()
+
+    def relay_step(j, p):
+        @pl.when(relay_level > j)
+        def _():
+            (relay_own(p) if j == 0 else relay_pass(j - 1, j, p)).wait_recv()
+            if j + 1 < half:
+                @pl.when(relay_level < half)
+                def _():
+                    relay_pass(j, j + 1, p).start()
+
+            @pl.when((relay_level < levels - 1) & (relay_level >= half))
+            def _():
+                relay_pass(j, j, p).start()
+
+            hand(j, p).start()
+
+    def right_wait(k):
+        for p in range(k * CHUNK // PIECE, (k + 1) * CHUNK // PIECE):
+            @pl.when(takes_back)
+            def _(p=p):
+                back_own(p).wait_recv()
+
+    acc[...] = jnp.full_like(acc, -1.0)
+    query_best[...] = jnp.full_like(query_best, -1.0)
+    for k in range(chunks):
+        unit_chunk(0, k)
+
+    near, far = (0, 1), (2, 3)
+    level_own(2, count).wait_recv()
+    level_pass(count).start()
+    level_own(1, count).wait_recv()
+    left_step(0, count)
+
+    @pl.when(takes_back)
+    def _():
+        back_own(count).wait_recv()
+
+    shift = len(direct)
+    for t in range(count):
+        if t < len(direct):
+            left_step(0, direct[t])
+        elif t - shift < len(direct):
+            if t == shift:
+                left_step(1, count)
+            left_step(1, direct[t - shift])
+        if t < len(detour):
+            ferry_step(detour[t])
+        if 0 <= t - 2 < len(detour):
+            relay_step(0, detour[t - 2])
+        if 0 <= t - shift < len(detour):
+            relay_step(1, detour[t - shift])
+        level_own(2, t).wait_recv()
+        level_pass(t).start()
+        if t == 0:
+            own_level(0)
+        if t == 2:
+            for p in range(count):
+                level_own(1, p).wait_recv()
+            for k in range(chunks):
+                unit_chunk(1, k)
+        if t == 3:
+            earlier_level(1)
+        if t == 4:
+            from_left(0, 0, near)
+        if t == 5:
+            right_wait(0)
+            from_right(0, near)
+        if t == 6:
+            left_rest(0, 1)
+            from_left(0, 1, near)
+        if t == 7:
+            right_wait(1)
+            from_right(1, near)
+        if t % 2:
+            unit_chunk(2, t // 2)
+    level_pass(count).wait_recv()
+    for t in range(count, shift + len(direct)):
+        left_step(1, direct[t - shift])
+        k = t - count
+        if k == 0:
+            earlier_level(2)
+        if k == 1:
+            left_rest(0, 2)
+            from_left(0, 2, near)
+    for p in range(count):
+        level_pass(p).wait_recv()
+    for k in range(chunks):
+        unit_chunk(3, k)
+    earlier_level(3)
+    left_rest(0, 3)
+    from_left(0, 3, near)
+    for k in range(chunks):
+        from_left(0, k, far)
+    for k in range(chunks):
+        if k < 2:
+            from_right(k, far)
+        else:
+            right_wait(k)
+            from_right(k, near + far)
+    for k in range(chunks):
+        left_rest(1, k)
+        from_left(1, k, near + far)
+
+    def res_copy(slot):
+        return pltpu.make_async_remote_copy(
+            src_ref=part.at[slot - 1], dst_ref=res.at[slot - 1], send_sem=res_send.at[slot - 1],
+            recv_sem=res_recv.at[slot - 1], device_id={"dom": plane, "wide": peer(slot)},
+            device_id_type=MESH)
+
+    def back_copy(which, source, wanted):
+        return pltpu.make_async_remote_copy(
+            src_ref=back.at[which], dst_ref=back_in.at[source - 1], send_sem=back_send.at[which],
+            recv_sem=back_recv.at[source - 1], device_id={"dom": plane, "wide": at_level(wanted)},
+            device_id_type=MESH)
+
+    def backs(act):
+        @pl.when(up & takes_back)
+        def _():
+            act(half, half, half + 1)
+
+        for source in range(1, levels):
+            for j in range(min(source, half)):
+                @pl.when(jnp.logical_not(up) & (level == source))
+                def _(source=source, j=j):
+                    act(j, source, min(source, half) - 1 - j)
+
+    def back_start(which, source, wanted):
+        back[which] = jnp.max(query_best[which], axis=0, keepdims=True)
+        back_copy(which, source, wanted).start()
+
+    backs(back_start)
+    for slot in (3, 2, 1):
+        part[slot - 1] = jnp.max(acc[slot], axis=0, keepdims=True)
+        res_copy(slot).start()
+    out_ref[...] = jnp.max(acc[0], axis=0, keepdims=True)
+    for slot in range(1, LANES):
+        res_copy(slot).wait_recv()
+        out_ref[...] = jnp.maximum(out_ref[...], res[slot - 1])
+
+    def take(source):
+        back_copy(0, source, 0).wait_recv()
+        out_ref[...] = jnp.maximum(out_ref[...], back_in[source - 1])
+
+    @pl.when(up & gives_back)
+    def _():
+        take(half)
+
+    for source in range(1, levels):
+        @pl.when(jnp.logical_not(up) & (level < min(source, half)))
+        def _(source=source):
+            take(source)
+
+    backs(lambda which, source, wanted: back_copy(which, source, wanted).wait_send())
+    for slot in range(1, LANES):
+        res_copy(slot).wait_send()
+    for p in order:
+        level_own(2, p).wait_send()
+        level_own(1, p).wait_send()
+        level_pass(p).wait_send()
+
+        @pl.when(sends_own)
+        def _(p=p):
+            (ferry_out if p in detour else next_own)(p).wait_send()
+
+        @pl.when(gives_back)
+        def _(p=p):
+            back_own(p).wait_send()
+
+        for j in range(half):
+            if p in detour:
+                @pl.when(relay_level > j)
+                def _(j=j, p=p):
+                    hand(j, p).wait_send()
+
+                if j + 1 < half:
+                    @pl.when((relay_level < half) & (relay_level > j))
+                    def _(j=j, p=p):
+                        relay_pass(j, j + 1, p).wait_send()
+
+                @pl.when((relay_level < levels - 1) & (relay_level >= half))
+                def _(j=j, p=p):
+                    relay_pass(j, j, p).wait_send()
+            else:
+                if j + 1 < half:
+                    @pl.when(sends_own & (level > j))
+                    def _(j=j, p=p):
+                        next_pass(j, j + 1, p).wait_send()
+
+                @pl.when(has_next & jnp.logical_not(sends_own))
+                def _(j=j, p=p):
+                    next_pass(j, j, p).wait_send()
+        if p in detour:
+            @pl.when(relay_level < half)
+            def _(p=p):
+                relay_own(p).wait_send()
+
+
+def grid_plan(levels, embeddings, cluster_id):
+    rows, width = embeddings.shape
+    half = levels // 2
+    pieces = rows // PIECE + 1
+    bf16, i32, f32 = jnp.bfloat16, jnp.int32, jnp.float32
+    dma = pltpu.SemaphoreType.DMA
+    vmem = pltpu.VMEM
+    best = pl.pallas_call(
+        functools.partial(grid_kernel, levels),
+        out_shape=jax.ShapeDtypeStruct((1, rows), f32),
+        in_specs=[pl.BlockSpec(memory_space=vmem)] * 2,
+        out_specs=pl.BlockSpec(memory_space=vmem),
+        scratch_shapes=[
+            vmem((LANES - 1, rows, width), bf16), vmem((LANES - 1, 1, rows), i32),
+            vmem((LANES, rows, width), bf16), vmem((LANES, rows, CHUNK), i32),
+            vmem((half, rows, width), bf16), vmem((half, 1, rows), i32),
+            vmem((rows, width), bf16), vmem((1, rows), i32),
+            vmem((rows, width), bf16), vmem((half, rows, width), bf16),
+            vmem((LANES, 8, rows), f32), vmem((half + 1, 8, rows), f32),
+            vmem((LANES - 1, 1, rows), f32), vmem((LANES - 1, 1, rows), f32),
+            vmem((half + 1, 1, rows), f32), vmem((levels - 1, 1, rows), f32),
+            dma((LANES - 1, pieces)), dma((LANES - 1, pieces)),
+            dma((half, pieces)), dma((half, pieces)),
+            dma((pieces,)), dma((pieces,)),
+            dma((pieces,)), dma((pieces,)),
+            dma((half, pieces)), dma((half, pieces)), dma((half, pieces)),
+            dma((LANES - 1,)), dma((LANES - 1,)),
+            dma((half + 1,)), dma((levels - 1,)),
+        ],
+        compiler_params=pltpu.CompilerParams(
+            collective_id=0, has_side_effects=True, vmem_limit_bytes=40 * 2**20),
+    )(embeddings, cluster_id.reshape(1, rows))
+    return best.reshape(-1)
+
+
 def solution(mesh):
     placed = (P(("dom", "wide"), None), P(("dom", "wide"), None))
+    levels = mesh.shape["wide"] // LANES
+    fits = levels == 4 and mesh.shape["wide"] % LANES == 0 and mesh.shape["dom"] == 2
+    plan = functools.partial(grid_plan, levels) if fits else per_device
     return jax.shard_map(
-        per_device, mesh=mesh, in_specs=placed, out_specs=P(("dom", "wide")), check_vma=False
+        plan, mesh=mesh, in_specs=placed, out_specs=P(("dom", "wide")), check_vma=False
     )

time: 120 us -> 59.3 us (0.49)
  the two profiles are of different devices: /device:TPU:0 before, /device:TPU:4 now
where the time goes in v2:
time: 59.3 us; the launch traced here: 59.1 us
  Pallas kernels  56.7 us (96%)
  local copies, waits for them, and re-layouts  2.39 us (4%)
    pallas_call x1, Pallas kernels, grid_plan(): pl.pallas_call(functools.partial(grid_kernel, levels), out_shape=jax.Shap...  56.7 us
    unnamed x5, local copies, waits for them, and re-layouts  2.39 us

profile of v2, /device:TPU:4, one launch (start us, length us, event | category | flops | bytes accessed | tf_op | source)
XLA Modules:
  0.0 59.1 jit_solution(766004092312424204)
XLA Ops:
  0.0 0.0 copy-start
  0.0 1.1 %copy-done = bf16[512,768]{1,0:T(8,128)(2,1)S(1)} copy-done((bf16[512,768]{1,0:T(8,128)(2,1)S(1)}, bf16[512,768]{1,0:T(8,128)(2,1)}, u32[]{:S(2)}) %copy-start) | copy-done | bytes 786456
  1.1 0.0 copy-start.1
  1.1 0.7 %copy-done.1 = s32[512,1]{0,1:T(1,128)S(1)} copy-done((s32[512,1]{0,1:T(1,128)S(1)}, s32[512,1]{0,1:T(1,128)}, u32[]{:S(2)}) %copy-start.1) | copy-done | bytes 2072
  1.8 56.7 %shard_map.28 = f32[1,512]{1,0:T(1,128)S(1)} custom-call(bf16[512,768]{1,0:T(8,128)(2,1)S(1)} %copy-done, s32[1,512]{1,0:T(1,128)S(1)} %bitcast.3), custom_call_target="tpu_custom_call" | custom-call | tf_op jit(solution)/shard_map/pallas_call | solution.py:546
  58.6 0.6 copy.4
Async XLA Ops:
  0.0 1.1 %copy-start = (bf16[512,768]{1,0:T(8,128)(2,1)S(1)}, bf16[512,768]{1,0:T(8,128)(2,1)}, u32[]{:S(2)}) copy-start(bf16[512,768]{1,0:T(8,128)(2,1)} %x_ref.1) | copy-start | bytes 2359300
  1.1 0.7 %copy-start.1 = (s32[512,1]{0,1:T(1,128)S(1)}, s32[512,1]{0,1:T(1,128)}, u32[]{:S(2)}) copy-start(s32[512,1]{0,1:T(1,128)} %param.3) | copy-start | bytes 6148

commit v3 on v2

--- a/solution.py
+++ b/solution.py
@@ -129,30 +129,17 @@
 
 
 def grid_kernel(levels, x_ref, id_ref, out_ref, lev, lev_id, unit, id_col, left, left_id, right,
-                right_id, ferry, relay, acc, query_best, part, res, back, back_in,
+                right_id, acc, query_best, part, res, back, back_in,
                 lev_send, lev_recv, left_send, left_recv, right_send, right_recv,
-                ferry_send, ferry_recv, relay_send, relay_recv, hand_send,
                 res_send, res_recv, back_send, back_recv):
-    plane = lax.axis_index("dom")
-    other = 1 - plane
     me = lax.axis_index("wide")
     lane = lax.rem(me, LANES)
-    place = me // LANES
-    base = place * LANES
+    level = me // LANES
+    base = level * LANES
     half = levels // 2
     rows, width = x_ref.shape
     count = rows // PIECE
     chunks = rows // CHUNK
-    up = plane == 0
-    level = jnp.where(up, place, levels - 1 - place)
-    step = jnp.where(up, LANES, -LANES)
-    relay_level = levels - 1 - level
-    detour = [p for p in range(count) if p % 2 and p > 1]
-    direct = [p for p in range(count) if p not in detour]
-
-    def at_level(wanted):
-        return me + (wanted - level) * step
-
     def peer(slot):
         low = lax.rem(lane, 2)
         high = lane // 2
@@ -167,25 +154,29 @@
 
     barrier = pltpu.get_barrier_semaphore()
     for slot in range(1, LANES):
-        pl.semaphore_signal(barrier, inc=1, device_id={"dom": plane, "wide": peer(slot)},
-                            device_id_type=MESH)
-    for far in range(1, levels):
-        there = lax.rem(place + far, levels) * LANES + lane
-        pl.semaphore_signal(barrier, inc=1, device_id={"dom": plane, "wide": there},
-                            device_id_type=MESH)
-    pl.semaphore_signal(barrier, inc=1, device_id={"dom": other, "wide": me}, device_id_type=MESH)
-    pl.semaphore_wait(barrier, LANES + levels - 1)
+        pl.semaphore_signal(barrier, inc=1, device_id={"wide": peer(slot)}, device_id_type=MESH)
+
+    @pl.when(has_next)
+    def _():
+        pl.semaphore_signal(barrier, inc=1, device_id={"wide": me + LANES}, device_id_type=MESH)
+
+    @pl.when(level > 0)
+    def _():
+        pl.semaphore_signal(barrier, inc=1, device_id={"wide": me - LANES}, device_id_type=MESH)
+
+    peers = LANES - 1 + has_next.astype(jnp.int32) + (level > 0).astype(jnp.int32)
+    pl.semaphore_wait(barrier, peers)
 
     def piece(block, ids, p):
         return ids if p == count else block.at[pl.ds(p * PIECE, PIECE)]
 
     order = [count] + list(range(count))
 
-    def send(src, src_id, dst, dst_id, p, ssem, rsem, dev, row=None):
+    def send(src, src_id, dst, dst_id, p, ssem, rsem, dev):
         return pltpu.make_async_remote_copy(
             src_ref=piece(src, src_id, p), dst_ref=piece(dst, dst_id, p),
             send_sem=ssem.at[p], recv_sem=rsem.at[p],
-            device_id={"dom": plane if row is None else row, "wide": dev}, device_id_type=MESH)
+            device_id={"wide": dev}, device_id_type=MESH)
 
     def level_own(slot, p):
         return send(x_ref, id_ref, lev.at[slot - 1], lev_id.at[slot - 1], p,
@@ -197,34 +188,19 @@
 
     def next_own(p):
         return send(x_ref, id_ref, left.at[0], left_id.at[0], p,
-                    left_send.at[0], left_recv.at[0], me + step)
+                    left_send.at[0], left_recv.at[0], me + LANES)
 
     def next_pass(j, to, p):
         return send(left.at[j], left_id.at[j], left.at[to], left_id.at[to], p,
-                    left_send.at[to], left_recv.at[to], me + step)
+                    left_send.at[to], left_recv.at[to], me + LANES)
 
     def back_own(p):
-        return send(x_ref, id_ref, right, right_id, p, right_send, right_recv, me - step)
-
-    def ferry_out(p):
-        return send(x_ref, None, ferry, None, p, ferry_send, ferry_recv, me, other)
-
-    def relay_own(p):
-        return send(ferry, None, relay.at[0], None, p, relay_send.at[0], relay_recv.at[0],
-                    me - step)
-
-    def relay_pass(j, to, p):
-        return send(relay.at[j], None, relay.at[to], None, p, relay_send.at[to],
-                    relay_recv.at[to], me - step)
-
-    def hand(j, p):
-        return send(relay.at[j], None, left.at[j], None, p, hand_send.at[j], left_recv.at[j],
-                    me, other)
+        return send(x_ref, id_ref, right, right_id, p, right_send, right_recv, me - LANES)
 
     for p in order:
         @pl.when(sends_own)
         def _(p=p):
-            (ferry_out if p in detour else next_own)(p).start()
+            next_own(p).start()
 
         level_own(2, p).start()
         level_own(1, p).start()
@@ -283,33 +259,25 @@
             value = jnp.where(key_ids == ids_of(slot)[...], value, -1.0)
             acc[slot] = jnp.maximum(acc[slot], fold(value))
 
-    def as_queries(block, ids, best_at, k, slots):
+    def as_queries(block, ids, k, slots):
         queries = normal(block[pl.ds(k * CHUNK, CHUNK), :])
         query_ids = ids[:, k * CHUNK:(k + 1) * CHUNK]
-        best = query_best[best_at, :, k * CHUNK:(k + 1) * CHUNK]
+        best = query_best[:, k * CHUNK:(k + 1) * CHUNK]
         for slot in slots:
             value = scores(unit[slot], queries)
             value = jnp.where(id_col[slot] == query_ids, value, -1.0)
             best = jnp.maximum(best, fold(value))
-        query_best[best_at, :, k * CHUNK:(k + 1) * CHUNK] = best
+        query_best[:, k * CHUNK:(k + 1) * CHUNK] = best
 
     def from_left(j, k, slots):
-        @pl.when((level > j) & up)
+        @pl.when(level > j)
         def _():
             as_keys(left.at[j], left_id.at[j], k, slots)
 
-        @pl.when((level > j) & jnp.logical_not(up))
+    def from_right(k, slots):
+        @pl.when(takes_back)
         def _():
-            as_queries(left.at[j], left_id.at[j], j, k, slots)
-
-    def from_right(k, slots):
-        @pl.when(takes_back & up)
-        def _():
-            as_queries(right, right_id, half, k, slots)
-
-        @pl.when(takes_back & jnp.logical_not(up))
-        def _():
-            as_keys(right, right_id, k, slots)
+            as_queries(right, right_id, k, slots)
 
     def left_wait(j, p):
         (next_own(p) if j == 0 else next_pass(j - 1, j, p)).wait_recv()
@@ -327,34 +295,6 @@
             def _():
                 next_pass(j, j, p).start()
 
-    def left_rest(j, k):
-        for p in detour:
-            if p * PIECE // CHUNK == k:
-                @pl.when(level > j)
-                def _(p=p):
-                    left_wait(j, p)
-
-    def ferry_step(p):
-        @pl.when(relay_level < half)
-        def _():
-            ferry_out(p).wait_recv()
-            relay_own(p).start()
-
-    def relay_step(j, p):
-        @pl.when(relay_level > j)
-        def _():
-            (relay_own(p) if j == 0 else relay_pass(j - 1, j, p)).wait_recv()
-            if j + 1 < half:
-                @pl.when(relay_level < half)
-                def _():
-                    relay_pass(j, j + 1, p).start()
-
-            @pl.when((relay_level < levels - 1) & (relay_level >= half))
-            def _():
-                relay_pass(j, j, p).start()
-
-            hand(j, p).start()
-
     def right_wait(k):
         for p in range(k * CHUNK // PIECE, (k + 1) * CHUNK // PIECE):
             @pl.when(takes_back)
@@ -366,6 +306,16 @@
     for k in range(chunks):
         unit_chunk(0, k)
 
+    def res_copy(slot):
+        return pltpu.make_async_remote_copy(
+            src_ref=part.at[slot - 1], dst_ref=res.at[slot - 1], send_sem=res_send.at[slot - 1],
+            recv_sem=res_recv.at[slot - 1], device_id={"wide": peer(slot)}, device_id_type=MESH)
+
+    def back_copy():
+        return pltpu.make_async_remote_copy(
+            src_ref=back, dst_ref=back_in, send_sem=back_send, recv_sem=back_recv,
+            device_id={"wide": me + LANES}, device_id_type=MESH)
+
     near, far = (0, 1), (2, 3)
     level_own(2, count).wait_recv()
     level_pass(count).start()
@@ -376,20 +326,8 @@
     def _():
         back_own(count).wait_recv()
 
-    shift = len(direct)
     for t in range(count):
-        if t < len(direct):
-            left_step(0, direct[t])
-        elif t - shift < len(direct):
-            if t == shift:
-                left_step(1, count)
-            left_step(1, direct[t - shift])
-        if t < len(detour):
-            ferry_step(detour[t])
-        if 0 <= t - 2 < len(detour):
-            relay_step(0, detour[t - 2])
-        if 0 <= t - shift < len(detour):
-            relay_step(1, detour[t - shift])
+        left_step(0, t)
         level_own(2, t).wait_recv()
         level_pass(t).start()
         if t == 0:
@@ -401,75 +339,59 @@
                 unit_chunk(1, k)
         if t == 3:
             earlier_level(1)
+            from_left(0, 0, near)
         if t == 4:
-            from_left(0, 0, near)
-        if t == 5:
             right_wait(0)
             from_right(0, near)
-        if t == 6:
-            left_rest(0, 1)
+        if t == 5:
             from_left(0, 1, near)
-        if t == 7:
             right_wait(1)
             from_right(1, near)
+        if t == 6:
+            from_left(0, 2, near)
         if t % 2:
             unit_chunk(2, t // 2)
     level_pass(count).wait_recv()
-    for t in range(count, shift + len(direct)):
-        left_step(1, direct[t - shift])
-        k = t - count
-        if k == 0:
-            earlier_level(2)
-        if k == 1:
-            left_rest(0, 2)
-            from_left(0, 2, near)
     for p in range(count):
         level_pass(p).wait_recv()
-    for k in range(chunks):
-        unit_chunk(3, k)
-    earlier_level(3)
-    left_rest(0, 3)
-    from_left(0, 3, near)
-    for k in range(chunks):
-        from_left(0, k, far)
-    for k in range(chunks):
-        if k < 2:
-            from_right(k, far)
-        else:
-            right_wait(k)
-            from_right(k, near + far)
-    for k in range(chunks):
-        left_rest(1, k)
-        from_left(1, k, near + far)
-
-    def res_copy(slot):
-        return pltpu.make_async_remote_copy(
-            src_ref=part.at[slot - 1], dst_ref=res.at[slot - 1], send_sem=res_send.at[slot - 1],
-            recv_sem=res_recv.at[slot - 1], device_id={"dom": plane, "wide": peer(slot)},
-            device_id_type=MESH)
-
-    def back_copy(which, source, wanted):
-        return pltpu.make_async_remote_copy(
-            src_ref=back.at[which], dst_ref=back_in.at[source - 1], send_sem=back_send.at[which],
-            recv_sem=back_recv.at[source - 1], device_id={"dom": plane, "wide": at_level(wanted)},
-            device_id_type=MESH)
-
-    def backs(act):
-        @pl.when(up & takes_back)
-        def _():
-            act(half, half, half + 1)
-
-        for source in range(1, levels):
-            for j in range(min(source, half)):
-                @pl.when(jnp.logical_not(up) & (level == source))
-                def _(source=source, j=j):
-                    act(j, source, min(source, half) - 1 - j)
-
-    def back_start(which, source, wanted):
-        back[which] = jnp.max(query_best[which], axis=0, keepdims=True)
-        back_copy(which, source, wanted).start()
-
-    backs(back_start)
+    left_step(1, count)
+    for t in range(count):
+        left_step(1, t)
+        k = t // 2
+        if t == 0:
+            from_left(0, 3, near)
+            for at in range(chunks):
+                unit_chunk(3, at)
+        if t == 1:
+            earlier_level(2)
+            earlier_level(3)
+        if t == 2:
+            from_left(0, 0, far)
+            from_left(1, 0, near + far)
+        if t == 3:
+            from_left(0, 1, far)
+            from_right(0, far)
+        if t == 4:
+            from_left(0, 2, far)
+            from_right(1, far)
+        if t == 5:
+            from_left(0, 3, far)
+            from_left(1, 1, near + far)
+        if t == 6:
+            right_wait(2)
+            from_right(2, near + far)
+            from_left(1, 2, near + far)
+        if t == 7:
+            right_wait(3)
+            from_right(3, near + far)
+
+            @pl.when(takes_back)
+            def _():
+                back[...] = jnp.max(query_best[...], axis=0, keepdims=True)
+                back_copy().start()
+
+            from_left(1, 3, near + far)
+
     for slot in (3, 2, 1):
         part[slot - 1] = jnp.max(acc[slot], axis=0, keepdims=True)
         res_copy(slot).start()
@@ -478,20 +400,15 @@
         res_copy(slot).wait_recv()
         out_ref[...] = jnp.maximum(out_ref[...], res[slot - 1])
 
-    def take(source):
-        back_copy(0, source, 0).wait_recv()
-        out_ref[...] = jnp.maximum(out_ref[...], back_in[source - 1])
-
-    @pl.when(up & gives_back)
+    @pl.when(gives_back)
     def _():
-        take(half)
-
-    for source in range(1, levels):
-        @pl.when(jnp.logical_not(up) & (level < min(source, half)))
-        def _(source=source):
-            take(source)
-
-    backs(lambda which, source, wanted: back_copy(which, source, wanted).wait_send())
+        back_copy().wait_recv()
+        out_ref[...] = jnp.maximum(out_ref[...], back_in[...])
+
+    @pl.when(takes_back)
+    def _():
+        back_copy().wait_send()
+
     for slot in range(1, LANES):
         res_copy(slot).wait_send()
     for p in order:
@@ -501,39 +418,21 @@
 
         @pl.when(sends_own)
         def _(p=p):
-            (ferry_out if p in detour else next_own)(p).wait_send()
+            next_own(p).wait_send()
 
         @pl.when(gives_back)
         def _(p=p):
             back_own(p).wait_send()
 
         for j in range(half):
-            if p in detour:
-                @pl.when(relay_level > j)
+            if j + 1 < half:
+                @pl.when(sends_own & (level > j))
                 def _(j=j, p=p):
-                    hand(j, p).wait_send()
-
-                if j + 1 < half:
-                    @pl.when((relay_level < half) & (relay_level > j))
-                    def _(j=j, p=p):
-                        relay_pass(j, j + 1, p).wait_send()
-
-                @pl.when((relay_level < levels - 1) & (relay_level >= half))
-                def _(j=j, p=p):
-                    relay_pass(j, j, p).wait_send()
-            else:
-                if j + 1 < half:
-                    @pl.when(sends_own & (level > j))
-                    def _(j=j, p=p):
-                        next_pass(j, j + 1, p).wait_send()
-
-                @pl.when(has_next & jnp.logical_not(sends_own))
-                def _(j=j, p=p):
-                    next_pass(j, j, p).wait_send()
-        if p in detour:
-            @pl.when(relay_level < half)
-            def _(p=p):
-                relay_own(p).wait_send()
+                    next_pass(j, j + 1, p).wait_send()
+
+            @pl.when(has_next & jnp.logical_not(sends_own))
+            def _(j=j, p=p):
+                next_pass(j, j, p).wait_send()
 
 
 def grid_plan(levels, embeddings, cluster_id):
@@ -553,17 +452,14 @@
             vmem((LANES, rows, width), bf16), vmem((LANES, rows, CHUNK), i32),
             vmem((half, rows, width), bf16), vmem((half, 1, rows), i32),
             vmem((rows, width), bf16), vmem((1, rows), i32),
-            vmem((rows, width), bf16), vmem((half, rows, width), bf16),
-            vmem((LANES, 8, rows), f32), vmem((half + 1, 8, rows), f32),
+            vmem((LANES, 8, rows), f32), vmem((8, rows), f32),
             vmem((LANES - 1, 1, rows), f32), vmem((LANES - 1, 1, rows), f32),
-            vmem((half + 1, 1, rows), f32), vmem((levels - 1, 1, rows), f32),
+            vmem((1, rows), f32), vmem((1, rows), f32),
             dma((LANES - 1, pieces)), dma((LANES - 1, pieces)),
             dma((half, pieces)), dma((half, pieces)),
             dma((pieces,)), dma((pieces,)),
-            dma((pieces,)), dma((pieces,)),
-            dma((half, pieces)), dma((half, pieces)), dma((half, pieces)),
             dma((LANES - 1,)), dma((LANES - 1,)),
-            dma((half + 1,)), dma((levels - 1,)),
+            dma, dma,
         ],
         compiler_params=pltpu.CompilerParams(
             collective_id=0, has_side_effects=True, vmem_limit_bytes=40 * 2**20),
@@ -574,7 +470,7 @@
 def solution(mesh):
     placed = (P(("dom", "wide"), None), P(("dom", "wide"), None))
     levels = mesh.shape["wide"] // LANES
-    fits = levels == 4 and mesh.shape["wide"] % LANES == 0 and mesh.shape["dom"] == 2
+    fits = levels == 4 and mesh.shape["wide"] % LANES == 0
     plan = functools.partial(grid_plan, levels) if fits else per_device
     return jax.shard_map(
         plan, mesh=mesh, in_specs=placed, out_specs=P(("dom", "wide")), check_vma=False

time: 59.3 us -> 48.5 us (0.82)
  the two profiles are of different devices: /device:TPU:4 before, /device:TPU:24 now
where the time goes in v3:
time: 48.5 us; the launch traced here: 48.4 us
  Pallas kernels  46 us (95%)
  local copies, waits for them, and re-layouts  2.39 us (5%)
    pallas_call x1, Pallas kernels, grid_plan(): pl.pallas_call(functools.partial(grid_kernel, levels), out_shape=jax.Shap...  46 us
    unnamed x5, local copies, waits for them, and re-layouts  2.39 us

profile of v3, /device:TPU:24, one launch (start us, length us, event | category | flops | bytes accessed | tf_op | source)
XLA Modules:
  0.0 48.4 jit_solution(13249737171012322562)
XLA Ops:
  0.0 0.0 copy-start
  0.0 1.1 %copy-done = bf16[512,768]{1,0:T(8,128)(2,1)S(1)} copy-done((bf16[512,768]{1,0:T(8,128)(2,1)S(1)}, bf16[512,768]{1,0:T(8,128)(2,1)}, u32[]{:S(2)}) %copy-start) | copy-done | bytes 786456
  1.1 0.0 copy-start.1
  1.1 0.7 %copy-done.1 = s32[512,1]{0,1:T(1,128)S(1)} copy-done((s32[512,1]{0,1:T(1,128)S(1)}, s32[512,1]{0,1:T(1,128)}, u32[]{:S(2)}) %copy-start.1) | copy-done | bytes 2072
  1.8 46.0 %shard_map.28 = f32[1,512]{1,0:T(1,128)S(1)} custom-call(bf16[512,768]{1,0:T(8,128)(2,1)S(1)} %copy-done, s32[1,512]{1,0:T(1,128)S(1)} %bitcast.3), custom_call_target="tpu_custom_call" | custom-call | tf_op jit(solution)/shard_map/pallas_call | solution.py:445
  47.8 0.6 %copy.4 = f32[512]{0:T(512)} copy(f32[512]{0:T(512)S(1)} %bitcast.2) | data formatting | bytes 4096
Async XLA Ops:
  0.0 1.1 %copy-start = (bf16[512,768]{1,0:T(8,128)(2,1)S(1)}, bf16[512,768]{1,0:T(8,128)(2,1)}, u32[]{:S(2)}) copy-start(bf16[512,768]{1,0:T(8,128)(2,1)} %x_ref.1) | copy-start | bytes 2359300
  1.1 0.7 %copy-start.1 = (s32[512,1]{0,1:T(1,128)S(1)}, s32[512,1]{0,1:T(1,128)}, u32[]{:S(2)}) copy-start(s32[512,1]{0,1:T(1,128)} %param.3) | copy-start | bytes 6148

commit v4 on v3

--- a/solution.py
+++ b/solution.py
@@ -128,7 +128,7 @@
 MESH = pl.DeviceIdType.MESH
 
 
-def grid_kernel(levels, x_ref, id_ref, out_ref, lev, lev_id, unit, id_col, left, left_id, right,
+def grid_kernel(levels, x_ref, id_ref, out_ref, own, own_sem, lev, lev_id, unit, id_col, left, left_id, right,
                 right_id, acc, query_best, part, res, back, back_in,
                 lev_send, lev_recv, left_send, left_recv, right_send, right_recv,
                 res_send, res_recv, back_send, back_recv):
@@ -152,6 +152,8 @@
     takes_back = level == half
     gives_back = level == half + 1
 
+    own_copy = pltpu.make_async_copy(x_ref, own, own_sem)
+    own_copy.start()
     barrier = pltpu.get_barrier_semaphore()
     for slot in range(1, LANES):
         pl.semaphore_signal(barrier, inc=1, device_id={"wide": peer(slot)}, device_id_type=MESH)
@@ -231,7 +233,7 @@
 
     def unit_chunk(slot, k):
         at = pl.ds(k * CHUNK, CHUNK)
-        unit[slot, at, :] = normal(x_ref[at, :] if slot == 0 else lev[slot - 1, at, :])
+        unit[slot, at, :] = normal(own[at, :] if slot == 0 else lev[slot - 1, at, :])
         id_col[slot, at, :] = column(ids_of(slot), k)
 
     def own_level(slot):
@@ -251,9 +253,9 @@
         def _():
             own_level(slot)
 
-    def as_keys(block, ids, k, slots):
-        keys = normal(block[pl.ds(k * CHUNK, CHUNK), :])
-        key_ids = column(ids, k)[:, :1]
+    def as_keys(block, ids, k, slots, begin=0, size=CHUNK):
+        keys = normal(block[pl.ds(k * CHUNK + begin, size), :])
+        key_ids = column(ids, k)[begin:begin + size, :1]
         for slot in slots:
             value = scores(keys, unit[slot])
             value = jnp.where(key_ids == ids_of(slot)[...], value, -1.0)
@@ -269,10 +271,10 @@
             best = jnp.maximum(best, fold(value))
         query_best[:, k * CHUNK:(k + 1) * CHUNK] = best
 
-    def from_left(j, k, slots):
+    def from_left(j, k, slots, begin=0, size=CHUNK):
         @pl.when(level > j)
         def _():
-            as_keys(left.at[j], left_id.at[j], k, slots)
+            as_keys(left.at[j], left_id.at[j], k, slots, begin, size)
 
     def from_right(k, slots):
         @pl.when(takes_back)
@@ -301,6 +303,7 @@
             def _(p=p):
                 back_own(p).wait_recv()
 
+    own_copy.wait()
     acc[...] = jnp.full_like(acc, -1.0)
     query_best[...] = jnp.full_like(query_best, -1.0)
     for k in range(chunks):
@@ -380,17 +383,18 @@
         if t == 6:
             right_wait(2)
             from_right(2, near + far)
-            from_left(1, 2, near + far)
-        if t == 7:
             right_wait(3)
             from_right(3, near + far)
+            from_left(1, 2, near + far)
+            from_left(1, 3, near + far, 0, PIECE)
+        if t == 7:
 
             @pl.when(takes_back)
             def _():
                 back[...] = jnp.max(query_best[...], axis=0, keepdims=True)
                 back_copy().start()
 
-            from_left(1, 3, near + far)
+            from_left(1, 3, near + far, PIECE, PIECE)
 
     for slot in (3, 2, 1):
         part[slot - 1] = jnp.max(acc[slot], axis=0, keepdims=True)
@@ -445,9 +449,10 @@
     best = pl.pallas_call(
         functools.partial(grid_kernel, levels),
         out_shape=jax.ShapeDtypeStruct((1, rows), f32),
-        in_specs=[pl.BlockSpec(memory_space=vmem)] * 2,
+        in_specs=[pl.BlockSpec(memory_space=pl.ANY), pl.BlockSpec(memory_space=vmem)],
         out_specs=pl.BlockSpec(memory_space=vmem),
         scratch_shapes=[
+            vmem((rows, width), bf16), dma,
             vmem((LANES - 1, rows, width), bf16), vmem((LANES - 1, 1, rows), i32),
             vmem((LANES, rows, width), bf16), vmem((LANES, rows, CHUNK), i32),
             vmem((half, rows, width), bf16), vmem((half, 1, rows), i32),

time: 48.5 us -> 50.5 us (1.041)
  Pallas kernels: 46 us -> 47.9 us
    pallas_call x1, Pallas kernels: 46 us -> 47.9 us  [grid_plan(): pl.pallas_call(functools.partial(grid_kernel, levels), out_shape=jax.Shap...]
where the time goes in v4:
time: 50.5 us; the launch traced here: 50.3 us
  Pallas kernels  47.9 us (95%)
  local copies, waits for them, and re-layouts  2.39 us (5%)
    pallas_call x1, Pallas kernels, grid_plan(): pl.pallas_call(functools.partial(grid_kernel, levels), out_shape=jax.Shap...  47.9 us
    unnamed x5, local copies, waits for them, and re-layouts  2.39 us

profile of v4, /device:TPU:24, one launch (start us, length us, event | category | flops | bytes accessed | tf_op | source)
XLA Modules:
  0.0 50.3 jit_solution(7508918331879067746)
XLA Ops:
  0.0 0.0 copy-start
  0.0 1.1 %copy-done = bf16[512,768]{1,0:T(8,128)(2,1)S(1)} copy-done((bf16[512,768]{1,0:T(8,128)(2,1)S(1)}, bf16[512,768]{1,0:T(8,128)(2,1)}, u32[]{:S(2)}) %copy-start) | copy-done | bytes 786456
  1.1 0.0 copy-start.1
  1.1 0.7 %copy-done.1 = s32[512,1]{0,1:T(1,128)S(1)} copy-done((s32[512,1]{0,1:T(1,128)S(1)}, s32[512,1]{0,1:T(1,128)}, u32[]{:S(2)}) %copy-start.1) | copy-done | bytes 2072
  1.8 47.9 %shard_map.28 = f32[1,512]{1,0:T(1,128)S(1)} custom-call(bf16[512,768]{1,0:T(8,128)(2,1)S(1)} %copy-done, s32[1,512]{1,0:T(1,128)S(1)} %bitcast.3), custom_call_target="tpu_custom_call" | custom-call | tf_op jit(solution)/shard_map/pallas_call | solution.py:449
  49.8 0.6 %copy.4 = f32[512]{0:T(512)} copy(f32[512]{0:T(512)S(1)} %bitcast.2) | data formatting | bytes 4096
Async XLA Ops:
  0.0 1.1 %copy-start = (bf16[512,768]{1,0:T(8,128)(2,1)S(1)}, bf16[512,768]{1,0:T(8,128)(2,1)}, u32[]{:S(2)}) copy-start(bf16[512,768]{1,0:T(8,128)(2,1)} %x_ref.1) | copy-start | bytes 2359300
  1.1 0.7 %copy-start.1 = (s32[512,1]{0,1:T(1,128)S(1)}, s32[512,1]{0,1:T(1,128)}, u32[]{:S(2)}) copy-start(s32[512,1]{0,1:T(1,128)} %param.3) | copy-start | bytes 6148
